TPU v7x, 128 devices: a whole 4x4x4 slice. The times are simulated.
128 devices in a mesh: ctx: 32 (over z, x, core), exp: 4 (over y).
Axes of the slice: x: 4, y: 4, z: 4, core: 2. Of those that a mesh axis runs over, the one named last changes fastest.
Arguments:
- queries: bfloat16 [8192, 4096], P('ctx', 'exp'), may hold values from -6 to 6
- key_rows: bfloat16 [8192, 4096], P('ctx', 'exp'), may hold values from -6 to 6
- value_rows: bfloat16 [8192, 4096], P('ctx', 'exp'), may hold values from -6 to 6
- gate_rows: bfloat16 [8192, 4096], P('ctx', 'exp'), may hold values from -6 to 6
- decay_exp: int32 [32], P('exp'), may hold values from 5 to 16
- attn_gain: float32 [4096], P('exp'), may hold values from 0.1 to 1.9
- out_proj: bfloat16 [4096, 6144], P('exp'), may hold values from -0.09375 to 0.09375
- residual: bfloat16 [8192, 6144], P(('ctx', 'exp')), may hold values from -6 to 6
- norm_gain: float32 [6144], replicated, may hold values from 0.1 to 1.9
- routes: int32 [8192, 2], P('ctx'), may hold values from 0 to 31, as said below
- route_weights: float32 [8192, 2], P('ctx'), may hold values from 0.1 to 1
- w_gate: bfloat16 [4, 9216, 6144], P('exp', 'ctx'), may hold values from -0.078125 to 0.078125
- w_up: bfloat16 [4, 9216, 6144], P('exp', 'ctx'), may hold values from -0.078125 to 0.078125
- w_down: bfloat16 [4, 9216, 6144], P('exp', 'ctx'), may hold values from -0.0625 to 0.0625
Outputs:
- layer_out: bfloat16 [8192, 6144], P(('ctx', 'exp'))
Inputs may be any that keep to these rules, and one draw needn't show every extreme that they name: `routes`: A row's two entries differ. An expert e below 4 is named only in column e % 2. In every aligned block of 64 rows each expert below 4 is named at most 8 times, and some expert below 4 exactly 8 times.
All inputs are finite; a program needn't handle non-finite values.
Results may differ from a plain program's by a relative error of at most 0.018.
Values may be sent and summed in bfloat16 or wider, within the bound.
A program may use at most 128 MiB of HBM per device.

v0:
```python
import jax
import jax.numpy as jnp
from jax import lax
from jax.sharding import PartitionSpec as P

EPSILON = 1e-06


def prefix(shard, axis, combine, identity):
    size, index = (lax.axis_size(axis), lax.axis_index(axis))
    everything = jax.tree.map(
        lambda part, kind: lax.all_gather(part.astype(kind), axis),
        shard,
        (jnp.bfloat16, jnp.bfloat16),
    )
    start = jax.tree.map(
        lambda part, zero: jnp.broadcast_to(jnp.asarray(zero, part.dtype), part.shape),
        shard,
        identity,
    )

    def turn(k, before):
        reached = k < index
        new = combine(
            before, jax.tree.map(lambda part, own: part[k].astype(own.dtype), everything, shard)
        )
        return jax.tree.map(lambda a, b: jnp.where(reached, a, b), new, before)

    return lax.fori_loop(0, size, turn, start)


def span_local(queries, key_rows, value_rows, decay_exp):
    row_count = queries.shape[0]
    head_count = decay_exp.shape[0]
    head_width = queries.shape[1] // head_count
    query_heads = queries.reshape(row_count, head_count, head_width)
    key_heads = key_rows.reshape(row_count, head_count, head_width)
    value_heads = value_rows.reshape(row_count, head_count, head_width)
    decay_rates = jnp.exp2(-decay_exp.astype(jnp.float32))
    positions = jnp.arange(row_count, dtype=jnp.float32)
    offsets = positions[:, None] - positions[None, :]
    damping = jnp.where(
        offsets[None] >= 0.0,
        jnp.exp(-decay_rates[:, None, None] * jnp.maximum(offsets, 0.0)[None]),
        0.0,
    )
    scores = jnp.einsum("thd,shd->hts", query_heads, key_heads, preferred_element_type=jnp.float32)
    mixing = (scores * damping).astype(jnp.bfloat16)
    inner_part = jnp.einsum("hts,shd->thd", mixing, value_heads, preferred_element_type=jnp.float32)
    tail_decay = jnp.exp(-decay_rates[None, :] * (row_count - 1.0 - positions)[:, None])
    keyed_rows = (key_heads.astype(jnp.float32) * tail_decay[:, :, None]).astype(jnp.bfloat16)
    update = jnp.einsum("shd,she->hde", keyed_rows, value_heads, preferred_element_type=jnp.float32)
    carry_decay = jnp.exp(-decay_rates * row_count)
    lead_decay = jnp.exp(-decay_rates[None, :] * (positions + 1.0)[:, None])
    leading = query_heads.astype(jnp.float32) * lead_decay[:, :, None]
    return (inner_part, leading, update, carry_decay)


def join_states(earlier, later):
    return (earlier[0] * later[0], later[0][:, None, None] * earlier[1] + later[1])


def settle(inner_part, leading, prior_state, gate_rows, attn_gain):
    outer_part = jnp.einsum("thd,hde->the", leading, prior_state, precision=lax.Precision.HIGHEST)
    mixed_heads = inner_part + outer_part
    row_count, head_count, head_width = mixed_heads.shape
    mean_square = jnp.mean(mixed_heads * mixed_heads, axis=2, keepdims=True)
    normed_heads = mixed_heads * lax.rsqrt(mean_square + EPSILON)
    gain_heads = attn_gain.reshape(head_count, head_width)
    gate_heads = gate_rows.reshape(row_count, head_count, head_width).astype(jnp.float32)
    settled = (normed_heads * gain_heads * jax.nn.sigmoid(gate_heads)).astype(jnp.bfloat16)
    return settled.reshape(row_count, head_count * head_width)


def token_norm(hidden, norm_gain):
    mean_square = jnp.mean(hidden * hidden, axis=1, keepdims=True)
    return (hidden * lax.rsqrt(mean_square + EPSILON) * norm_gain).astype(jnp.bfloat16)


def slot_tables(owners, chosen_ids, weights, capacity):
    column = owners % 2
    chosen = jnp.where(column[:, None] == 0, chosen_ids[None, :, 0], chosen_ids[None, :, 1])
    weight_rows = jnp.where(column[:, None] == 0, weights[None, :, 0], weights[None, :, 1])
    picked = chosen == owners[:, None]
    slot_rank = jnp.cumsum(picked.astype(jnp.int32), axis=1) - 1
    slot_ids = jnp.arange(capacity, dtype=jnp.int32)
    slot_table = picked[:, None, :] & (slot_rank[:, None, :] == slot_ids[None, :, None])
    return (slot_table.astype(jnp.bfloat16), jnp.where(slot_table, weight_rows[:, None, :], 0.0))


def expert_part(slot_rows, gate_cols, up_cols, down_rows):
    contract_dims = (((1,), (1,)), ((), ()))
    first_half = lax.dot_general(
        slot_rows, gate_cols, contract_dims, preferred_element_type=jnp.float32
    )
    second_half = lax.dot_general(
        slot_rows, up_cols, contract_dims, preferred_element_type=jnp.float32
    )
    activated = (jax.nn.silu(first_half) * second_half).astype(jnp.bfloat16)
    return jnp.dot(activated, down_rows, preferred_element_type=jnp.float32)


def body(
    queries,
    key_rows,
    value_rows,
    gate_rows,
    decay_exp,
    attn_gain,
    out_proj,
    residual,
    norm_gain,
    routes,
    route_weights,
    w_gate,
    w_up,
    w_down,
):
    inner_part, leading, update, carry_decay = span_local(queries, key_rows, value_rows, decay_exp)
    head_count = decay_exp.shape[0]
    head_width = queries.shape[1] // head_count
    identity = (
        jnp.ones((head_count,), jnp.float32),
        jnp.zeros((head_count, head_width, head_width), jnp.float32),
    )
    carried, prior_state = prefix((carry_decay, update), "ctx", join_states, identity)
    settled = settle(inner_part, leading, prior_state, gate_rows, attn_gain)
    span_rows = queries.shape[0]
    group_count = lax.axis_size("exp")
    group_rows = span_rows // group_count
    group_index = lax.axis_index("exp")
    first_mine = group_index * group_rows
    capacity = group_rows // 8
    gate_cols = w_gate[0]
    up_cols = w_up[0]
    down_rows = w_down[0]
    placed = lax.dynamic_update_slice_in_dim(
        jnp.zeros((span_rows, residual.shape[1]), jnp.float32),
        residual.astype(jnp.float32),
        first_mine,
        0,
    )
    projected = jnp.dot(settled, out_proj, preferred_element_type=jnp.float32) + placed
    hidden_all = lax.psum(projected.astype(jnp.bfloat16), "exp").astype(jnp.float32)
    normed_all = token_norm(hidden_all, norm_gain)
    owners = jnp.reshape(group_index, (1,))
    slot_table, weighted = slot_tables(owners, routes, route_weights, capacity * group_count)
    outgoing = jnp.einsum(
        "ecn,nd->cd", slot_table, normed_all, preferred_element_type=jnp.float32
    ).astype(jnp.bfloat16)
    gathered = lax.all_gather(outgoing, "ctx", axis=0, tiled=True)
    produced = lax.psum_scatter(
        expert_part(gathered, gate_cols, up_cols, down_rows).astype(jnp.bfloat16),
        "ctx",
        scatter_dimension=0,
        tiled=True,
    ).astype(jnp.float32)
    spread_back = jnp.einsum("ecn,cd->nd", weighted, produced, precision=lax.Precision.HIGHEST)
    mixture = lax.psum_scatter(
        spread_back.astype(jnp.bfloat16), "exp", scatter_dimension=0, tiled=True
    ).astype(jnp.float32)
    hidden = lax.dynamic_slice_in_dim(hidden_all, first_mine, group_rows, 0)
    return (hidden + mixture).astype(jnp.bfloat16)


def solution(mesh):
    in_specs = (
        P("ctx", "exp"),
        P("ctx", "exp"),
        P("ctx", "exp"),
        P("ctx", "exp"),
        P("exp"),
        P("exp"),
        P("exp", None),
        P(("ctx", "exp"), None),
        P(),
        P("ctx", None),
        P("ctx", None),
        P("exp", "ctx", None),
        P("exp", "ctx", None),
        P("exp", "ctx", None),
    )
    out_specs = P(("ctx", "exp"), None)
    return jax.shard_map(body, mesh=mesh, in_specs=in_specs, out_specs=out_specs, check_vma=False)
```

profile of v0, /device:TPU:1, one launch (start us, length us, event | category | flops | bytes accessed | tf_op | source)
XLA Modules:
  0.0 523.0 jit_solution(2067149946234657723)
XLA Ops:
  7.9 2.1 copy.36
  10.7 2.2 convolution_convert_fusion.3
  15.6 65.4 %all-reduce = bf16[256]{0:T(256)(128)(2,1)S(1)} all-reduce(bf16[256]{0:T(256)(128)(2,1)S(1)} %dynamic-update-slice.1), channel_id=2, replica_groups=mesh['ctx'=32,'exp'=4] {'ctx'}, use_global_device_ids=true, to_apply=%add | all-reduce | flops 256 | bytes 1024
  81.7 2.3 add_divide_fusion
  84.0 2.6 copy.34
  88.1 86.4 %while.14 = (s32[]{:T(128)}, f32[8,128,128]{2,1,0:T(8,128)}, s32[]{:T(128)}, bf16[32,8]{1,0:T(8,128)(2,1)}, bf16[32,8,128,128]{3,2,1,0:T(8,128)(2,1)}, /*index=5*/s32[]{:T(128)}, s32[]{:T(128)}) while((s32[]{:T(128)}, f32[8,128,128]{2,1,0:T(8,128)}, s32[]{:T(128)}, bf16[32,8]{1,0:T(8,128)(2,1)}, ...), condition=%wide.region_1.2_spmd.clone, body=%wide.region_0.1_spmd.clone.sunk | while | flops 655372 | bytes 1310905 | solution.py:29
  91.3 2.0 fusion.70
  94.1 2.0 fusion.70
  96.8 2.0 fusion.70
  99.5 2.0 fusion.70
  102.2 2.0 fusion.70
  104.9 2.0 fusion.70
  107.7 2.0 fusion.70
  110.3 2.0 fusion.70
  113.0 2.0 fusion.70
  115.6 2.0 fusion.70
  118.3 2.0 fusion.70
  174.5 3.6 convolution_bitcast_fusion
  178.1 3.7 multiply_reduce_fusion.1
  183.6 6.7 %fusion.57 = f32[256,6144]{1,0:T(8,128)S(1)} fusion(bf16[256,1024]{0,1:T(8,128)(2,1)S(1)} %bitcast.89, bf16[1024,6144]{1,0:T(8,128)(2,1)} %param.22), kind=kOutput, calls=%fused_computation.78 | convolution fusion | flops 3221225472 | bytes 19398656 | tf_op jit(solution)/shard_map/dot_general | solution.py:143
  190.6 2.1 convert_element_type.110
  193.5 76.0 %all-reduce.3.cloned.1.call-done = bf16[256,6144]{1,0:T(8,128)(2,1)} async-done(((bf16[256,6144]{1,0:T(8,128)(2,1)}), bf16[256,6144]{1,0:T(8,128)(2,1)}) %all-reduce.3.cloned.1.call-update) | async-done | bytes 3145744 | tf_op jit(solution)/shard_map/psum | solution.py:144
  269.6 2.6 multiply_reduce_fusion
  272.2 3.7 convolution_convert_fusion.2
  276.1 63.1 %all-gather.5.cloned.1.call-done = bf16[1024,6144]{1,0:T(8,128)(2,1)} async-done(((bf16[32,6144]{1,0:T(8,128)(2,1)}), bf16[1024,6144]{1,0:T(8,128)(2,1)}) %all-gather.5.cloned.1.call-update) | async-done | bytes 12582928 | tf_op jit(solution)/shard_map/all_gather | solution.py:151
  339.2 10.5 %fusion.4 = f32[1024,288]{0,1:T(8,128)} fusion(bf16[1024,6144]{1,0:T(8,128)(2,1)} %all-gather.5.cloned.1.call-done, bf16[1,288,6144]{2,1,0:T(8,128)(2,1)} %param.27), kind=kOutput, calls=%fused_computation.11 | convolution fusion | flops 3623878656 | bytes 17301504 | tf_op jit(solution)/shard_map/dot_general | solution.py:93
  349.7 17.7 %convolution_convert_fusion = bf16[1024,6144]{1,0:T(8,128)(2,1)} fusion(bf16[1,288,6144]{2,1,0:T(8,128)(2,1)S(1)} %copy-done, bf16[1024,6144]{1,0:T(8,128)(2,1)} %all-gather.5.cloned.1.call-done, bf16[1,288,6144]{2,1,0:T(8,128)(2,1)} %param.28, f32[1024,288]{0,1:T(8,128)} %fusion.4), kind=kOutput, calls=%fused_computation.3 | convolution fusion | flops 7255818240 | bytes 33423360 | tf_op jit(solution)/shard_map/dot_general | solution.py:100
  368.0 101.9 %reduce-scatter.3.cloned.1.call-done = bf16[32,6144]{1,0:T(8,128)(2,1)} async-done(((bf16[1024,6144]{1,0:T(8,128)(2,1)}), bf16[32,6144]{1,0:T(8,128)(2,1)}) %reduce-scatter.3.cloned.1.call-update) | async-done | bytes 393232 | tf_op jit(solution)/shard_map/reduce_scatter | solution.py:152
  469.9 5.1 convolution_convert_fusion.1
  475.1 5.4 %convert_element_type.111 = f32[256,6144]{1,0:T(8,128)} convert(bf16[256,6144]{1,0:T(8,128)(2,1)} %all-reduce.3.cloned.1.call-done) | non-fusion elementwise | flops 1572864 | bytes 9437184 | tf_op jit(solution)/shard_map/convert_element_type | solution.py:144
  480.5 33.3 %reduce-scatter.5.cloned.1.call-done = bf16[64,6144]{1,0:T(8,128)(2,1)} async-done(((bf16[256,6144]{1,0:T(8,128)(2,1)}), bf16[64,6144]{1,0:T(8,128)(2,1)}) %reduce-scatter.5.cloned.1.call-update) | async-done | bytes 786448 | tf_op jit(solution)/shard_map/reduce_scatter | solution.py:159
  513.8 2.7 add_convert_fusion
  (101 shorter events, 74.2 us)
Async XLA Ops:
  6.5 343.1 %copy-start = (bf16[1,288,6144]{2,1,0:T(8,128)(2,1)S(1)}, bf16[1,288,6144]{2,1,0:T(8,128)(2,1)}, u32[]{:S(2)}) copy-start(bf16[1,288,6144]{2,1,0:T(8,128)(2,1)} %param.29) | copy-start | bytes 10616836
  6.5 81.6 %all-gather.7.cloned.1.call-start = ((), (), s32[]{:S(2)}) async-start(), calls=%async_computation.6 | async-start | bytes 8650752 | tf_op jit(solution)/shard_map/all_gather | solution.py:12
  12.9 256.7 %all-reduce.3.cloned.1.call-start = ((), (), s32[]{:S(2)}) async-start(), calls=%async_computation.2 | async-start | bytes 6291456 | tf_op jit(solution)/shard_map/psum | solution.py:144
  88.1 90.0 %copy-start.6 = (f32[8]{0:T(128)S(1)}, f32[8]{0:T(128)}, u32[]{:S(2)}) copy-start(f32[8]{0:T(128)} %get-tuple-element.131) | copy-start | bytes 100
  174.5 7.3 %copy-start.3 = (f32[1024]{0:T(1024)S(1)}, f32[1024]{0:T(1024)}, u32[]{:S(2)}) copy-start(f32[1024]{0:T(1024)} %param.21) | copy-start | bytes 12292
  183.6 6.7 %copy-start.2 = (bf16[64,6144]{1,0:T(8,128)(2,1)S(1)}, bf16[64,6144]{1,0:T(8,128)(2,1)}, u32[]{:S(2)}) copy-start(bf16[64,6144]{1,0:T(8,128)(2,1)} %param.23) | copy-start | bytes 2359300
  190.6 2.2 copy-start.5
  192.7 146.5 %all-gather.5.cloned.1.call-start = ((), (), s32[]{:S(2)}) async-start(), calls=%async_computation.3 | async-start | bytes 12976128 | tf_op jit(solution)/shard_map/all_gather | solution.py:151
  275.9 194.0 %reduce-scatter.3.cloned.1.call-start = ((), (), s32[]{:S(2)}) async-start(), calls=%async_computation.4 | async-start | bytes 12976128 | tf_op jit(solution)/shard_map/reduce_scatter | solution.py:152
  367.3 0.7 copy-start.4
  367.4 146.5 %reduce-scatter.5.cloned.1.call-start = ((), (), s32[]{:S(2)}) async-start(), calls=%async_computation.5 | async-start | bytes 3932160 | tf_op jit(solution)/shard_map/reduce_scatter | solution.py:159
  475.0 41.5 %copy-start.1 = (bf16[1,288,6144]{2,1,0:T(8,128)(2,1)S(1)}, bf16[1,288,6144]{2,1,0:T(8,128)(2,1)}, u32[]{:S(2)}) copy-start(bf16[1,288,6144]{2,1,0:T(8,128)(2,1)} %param.29) | copy-start | bytes 10616836
Sparse Core Ops, SparseCore 0:
  13.0 56.8 all-gather.6
  192.8 76.7 all-reduce.2
  276.0 63.1 all-gather.4
  367.5 102.3 reduce-scatter.2
  475.2 38.6 reduce-scatter.4
where the time goes:
time: 525 us; the launch traced here: 523 us
  waiting for transfers between devices  274 us (52%)
  other arithmetic  108 us (21%)
  blocking collectives  65.4 us (12%)
  matrix products  53 us (10%)
  between operations  13.8 us (3%)
  local copies, waits for them, and re-layouts  8.36 us (2%)
    reduce_scatter x1, waiting for transfers between devices, body(): lax.psum_scatter(expert_part(gathered, gate_cols, up_cols, down_rows).ast...  102 us
    psum x1, waiting for transfers between devices, body(): lax.psum(projected.astype(jnp.bfloat16), 'exp').astype(jnp.float32)  76 us
    unnamed x1, blocking collectives  65.4 us
    select_n x32, other arithmetic, turn(): return jax.tree.map(lambda a, b: jnp.where(reached, a, b), new, before)  65.1 us
    all_gather x1, waiting for transfers between devices, body(): gathered = lax.all_gather(outgoing, 'ctx', axis=0, tiled=True)  63.1 us
    reduce_scatter x1, waiting for transfers between devices, body(): lax.psum_scatter(spread_back.astype(jnp.bfloat16), 'exp', scatter_dimensi...  33.3 us
    convert_element_type x32, other arithmetic, turn(): part[k].astype(own.dtype)  21.3 us
    dot_general x1, matrix products, expert_part(): return jnp.dot(activated, down_rows, preferred_element_type=jnp.float32)  17.7 us
  transfers between devices with their start and end apart: 5, of which 4 were waited for; matrix products, arithmetic and copies ran while one was open for 3% of the time, Pallas kernels for 0%

commit v1 on v0

--- a/solution.py
+++ b/solution.py
@@ -141,7 +141,9 @@
         0,
     )
     projected = jnp.dot(settled, out_proj, preferred_element_type=jnp.float32) + placed
-    hidden_all = lax.psum(projected.astype(jnp.bfloat16), "exp").astype(jnp.float32)
+    hidden_all = jnp.sum(lax.all_gather(projected.astype(jnp.bfloat16), "exp"), axis=0).astype(
+        jnp.float32
+    )
     normed_all = token_norm(hidden_all, norm_gain)
     owners = jnp.reshape(group_index, (1,))
     slot_table, weighted = slot_tables(owners, routes, route_weights, capacity * group_count)

time: 525 us -> 579 us (1.10)
  waiting for transfers between devices: 274 us -> 319 us
  other arithmetic: 108 us -> 117 us
    all_gather x0 -> x1, waiting for transfers between devices: none -> 119 us  [body(): lax.all_gather(projected.astype(jnp.bfloat16), 'exp')]
    psum x1 -> x0, waiting for transfers between devices: 76 us -> none  [body(): lax.psum(projected.astype(jnp.bfloat16), 'exp').astype(jnp.float32)]
    reduce_sum x0 -> x1, other arithmetic: none -> 9.57 us  [body(): jnp.sum(lax.all_gather(projected.astype(jnp.bfloat16), 'exp'), axis=0)]
where the time goes in v1:
time: 579 us; the launch traced here: 577 us
  waiting for transfers between devices  319 us (55%)
  other arithmetic  117 us (20%)
  blocking collectives  65.4 us (11%)
  matrix products  53 us (9%)
  between operations  13.8 us (2%)
  local copies, waits for them, and re-layouts  8.36 us (1%)
    all_gather x1, waiting for transfers between devices, body(): lax.all_gather(projected.astype(jnp.bfloat16), 'exp')  119 us
    reduce_scatter x1, waiting for transfers between devices, body(): lax.psum_scatter(expert_part(gathered, gate_cols, up_cols, down_rows).ast...  102 us
    unnamed x1, blocking collectives  65.4 us
    select_n x32, other arithmetic, turn(): return jax.tree.map(lambda a, b: jnp.where(reached, a, b), new, before)  65.1 us
    all_gather x1, waiting for transfers between devices, body(): gathered = lax.all_gather(outgoing, 'ctx', axis=0, tiled=True)  64.3 us
    reduce_scatter x1, waiting for transfers between devices, body(): lax.psum_scatter(spread_back.astype(jnp.bfloat16), 'exp', scatter_dimensi...  33.4 us
    convert_element_type x32, other arithmetic, turn(): part[k].astype(own.dtype)  21.3 us
    dot_general x1, matrix products, expert_part(): return jnp.dot(activated, down_rows, preferred_element_type=jnp.float32)  17.7 us
  transfers between devices with their start and end apart: 5, of which 4 were waited for; matrix products, arithmetic and copies ran while one was open for 3% of the time, Pallas kernels for 0%

profile of v1, /device:TPU:1, one launch (start us, length us, event | category | flops | bytes accessed | tf_op | source)
XLA Modules:
  0.0 576.8 jit_solution(9405775109052293692)
XLA Ops:
  7.9 2.1 copy.36
  10.8 2.2 convolution_convert_fusion.3
  15.7 65.4 %all-reduce = bf16[256]{0:T(256)(128)(2,1)S(1)} all-reduce(bf16[256]{0:T(256)(128)(2,1)S(1)} %dynamic-update-slice.1), channel_id=2, replica_groups=mesh['ctx'=32,'exp'=4] {'ctx'}, use_global_device_ids=true, to_apply=%add | all-reduce | flops 256 | bytes 1024
  81.8 2.3 add_divide_fusion
  84.1 2.6 copy.34
  88.2 86.4 %while.14 = (s32[]{:T(128)}, f32[8,128,128]{2,1,0:T(8,128)}, s32[]{:T(128)}, bf16[32,8]{1,0:T(8,128)(2,1)}, bf16[32,8,128,128]{3,2,1,0:T(8,128)(2,1)}, /*index=5*/s32[]{:T(128)}, s32[]{:T(128)}) while((s32[]{:T(128)}, f32[8,128,128]{2,1,0:T(8,128)}, s32[]{:T(128)}, bf16[32,8]{1,0:T(8,128)(2,1)}, ...), condition=%wide.region_1.2_spmd.clone, body=%wide.region_0.1_spmd.clone.sunk | while | flops 655372 | bytes 1310905 | solution.py:29
  91.4 2.0 fusion.70
  94.1 2.0 fusion.70
  96.9 2.0 fusion.70
  99.6 2.0 fusion.70
  102.3 2.0 fusion.70
  105.0 2.0 fusion.70
  107.7 2.0 fusion.70
  110.4 2.0 fusion.70
  113.1 2.0 fusion.70
  115.7 2.0 fusion.70
  174.6 3.6 convolution_bitcast_fusion
  178.2 3.7 multiply_reduce_fusion.1
  183.7 6.7 %fusion.57 = f32[256,6144]{1,0:T(8,128)S(1)} fusion(bf16[256,1024]{0,1:T(8,128)(2,1)S(1)} %bitcast.91, bf16[1024,6144]{1,0:T(8,128)(2,1)} %param.22), kind=kOutput, calls=%fused_computation.78 | convolution fusion | flops 3221225472 | bytes 19398656 | tf_op jit(solution)/shard_map/dot_general | solution.py:143
  190.7 2.1 convert_element_type.112
  193.6 118.9 %all-gather.11.cloned.1.call-done = bf16[1024,6144]{1,0:T(8,128)(2,1)} async-done(((bf16[256,6144]{1,0:T(8,128)(2,1)}), bf16[1024,6144]{1,0:T(8,128)(2,1)}) %all-gather.11.cloned.1.call-update) | async-done | bytes 12582928 | tf_op jit(solution)/shard_map/all_gather | solution.py:144
  312.6 9.6 %reduce_sum.34 = bf16[256,6144]{1,0:T(8,128)(2,1)} reduce(bf16[4,256,6144]{2,1,0:T(8,128)(2,1)} %bitcast.89, bf16[]{:T(256)} %constant.86.clone.1), dimensions={0}, to_apply=%region_3.4 | reduce | flops 4718592 | bytes 15728642 | tf_op jit(solution)/shard_map/reduce_sum | solution.py:144
  322.1 2.6 multiply_reduce_fusion
  324.7 3.7 convolution_convert_fusion.2
  328.6 64.3 %all-gather.7.cloned.1.call-done = bf16[1024,6144]{1,0:T(8,128)(2,1)} async-done(((bf16[32,6144]{1,0:T(8,128)(2,1)}), bf16[1024,6144]{1,0:T(8,128)(2,1)}) %all-gather.7.cloned.1.call-update) | async-done | bytes 12582928 | tf_op jit(solution)/shard_map/all_gather | solution.py:153
  392.9 10.5 %fusion.4 = f32[1024,288]{0,1:T(8,128)} fusion(bf16[1024,6144]{1,0:T(8,128)(2,1)} %all-gather.7.cloned.1.call-done, bf16[1,288,6144]{2,1,0:T(8,128)(2,1)} %param.27), kind=kOutput, calls=%fused_computation.11 | convolution fusion | flops 3623878656 | bytes 17301504 | tf_op jit(solution)/shard_map/dot_general | solution.py:93
  403.4 17.7 %convolution_convert_fusion = bf16[1024,6144]{1,0:T(8,128)(2,1)} fusion(bf16[1,288,6144]{2,1,0:T(8,128)(2,1)S(1)} %copy-done, bf16[1024,6144]{1,0:T(8,128)(2,1)} %all-gather.7.cloned.1.call-done, bf16[1,288,6144]{2,1,0:T(8,128)(2,1)} %param.28, f32[1024,288]{0,1:T(8,128)} %fusion.4), kind=kOutput, calls=%fused_computation.3 | convolution fusion | flops 7255818240 | bytes 33423360 | tf_op jit(solution)/shard_map/dot_general | solution.py:100
  421.7 101.9 %reduce-scatter.3.cloned.1.call-done = bf16[32,6144]{1,0:T(8,128)(2,1)} async-done(((bf16[1024,6144]{1,0:T(8,128)(2,1)}), bf16[32,6144]{1,0:T(8,128)(2,1)}) %reduce-scatter.3.cloned.1.call-update) | async-done | bytes 393232 | tf_op jit(solution)/shard_map/reduce_scatter | solution.py:154
  523.6 5.1 convolution_convert_fusion.1
  528.8 5.4 convert_element_type.113
  534.2 33.4 %reduce-scatter.5.cloned.1.call-done = bf16[64,6144]{1,0:T(8,128)(2,1)} async-done(((bf16[256,6144]{1,0:T(8,128)(2,1)}), bf16[64,6144]{1,0:T(8,128)(2,1)}) %reduce-scatter.5.cloned.1.call-update) | async-done | bytes 786448 | tf_op jit(solution)/shard_map/reduce_scatter | solution.py:161
  567.6 2.7 add_convert_fusion
  (102 shorter events, 76.3 us)
Async XLA Ops:
  6.5 396.8 %copy-start = (bf16[1,288,6144]{2,1,0:T(8,128)(2,1)S(1)}, bf16[1,288,6144]{2,1,0:T(8,128)(2,1)}, u32[]{:S(2)}) copy-start(bf16[1,288,6144]{2,1,0:T(8,128)(2,1)} %param.29) | copy-start | bytes 10616836
  6.5 81.6 %all-gather.9.cloned.1.call-start = ((), (), s32[]{:S(2)}) async-start(), calls=%async_computation.5 | async-start | bytes 8650752 | tf_op jit(solution)/shard_map/all_gather | solution.py:12
  13.0 299.6 %all-gather.11.cloned.1.call-start = ((), (), s32[]{:S(2)}) async-start(), calls=%async_computation.6 | async-start | bytes 15728640 | tf_op jit(solution)/shard_map/all_gather | solution.py:144
  88.2 90.0 %copy-start.6 = (f32[8]{0:T(128)S(1)}, f32[8]{0:T(128)}, u32[]{:S(2)}) copy-start(f32[8]{0:T(128)} %get-tuple-element.131) | copy-start | bytes 100
  174.6 7.3 %copy-start.3 = (f32[1024]{0:T(1024)S(1)}, f32[1024]{0:T(1024)}, u32[]{:S(2)}) copy-start(f32[1024]{0:T(1024)} %param.21) | copy-start | bytes 12292
  183.7 6.7 %copy-start.2 = (bf16[64,6144]{1,0:T(8,128)(2,1)S(1)}, bf16[64,6144]{1,0:T(8,128)(2,1)}, u32[]{:S(2)}) copy-start(bf16[64,6144]{1,0:T(8,128)(2,1)} %param.23) | copy-start | bytes 2359300
  190.7 2.2 copy-start.5
  192.8 200.1 %all-gather.7.cloned.1.call-start = ((), (), s32[]{:S(2)}) async-start(), calls=%async_computation.2 | async-start | bytes 12976128 | tf_op jit(solution)/shard_map/all_gather | solution.py:153
  328.4 195.2 %reduce-scatter.3.cloned.1.call-start = ((), (), s32[]{:S(2)}) async-start(), calls=%async_computation.3 | async-start | bytes 12976128 | tf_op jit(solution)/shard_map/reduce_scatter | solution.py:154
  421.0 0.7 copy-start.4
  421.1 146.5 %reduce-scatter.5.cloned.1.call-start = ((), (), s32[]{:S(2)}) async-start(), calls=%async_computation.4 | async-start | bytes 3932160 | tf_op jit(solution)/shard_map/reduce_scatter | solution.py:161
  528.7 41.5 %copy-start.1 = (bf16[1,288,6144]{2,1,0:T(8,128)(2,1)S(1)}, bf16[1,288,6144]{2,1,0:T(8,128)(2,1)}, u32[]{:S(2)}) copy-start(bf16[1,288,6144]{2,1,0:T(8,128)(2,1)} %param.29) | copy-start | bytes 10616836
Sparse Core Ops, SparseCore 0:
  13.1 56.8 all-gather.8
  192.9 119.6 all-gather.10
  328.5 64.3 all-gather.6
  421.2 102.3 reduce-scatter.2
  528.9 38.6 reduce-scatter.4
